TPU v7x, 256 devices: a whole 4x4x8 slice. The times are simulated.
256 devices in a mesh: ctx: 64 (over x_hi, y, z), tp: 4 (over x_lo, core).
Axes of the slice: x: 4 (x_hi: 2, x_lo: 2; x = x_hi * 2 + x_lo), y: 4, z: 8, core: 2. Of those that a mesh axis runs over, the one named last changes fastest.
Arguments:
- hidden: bfloat16 [32768, 5120], P('ctx', 'tp'), may hold values from -6 to 6
- queries: bfloat16 [32768, 5120], P('ctx', 'tp'), may hold values from -600 to 600
- lengths: int32 [256], replicated, may hold values from 1 to 2048, 32768 in all
- norm_gain: float32 [5120], P('tp'), may hold values from 0.5 to 1.5
- kv_weight: bfloat16 [5120, 2, 1024], P(None, None, 'tp'), may hold values from -0.078125 to 0.078125
- kv_bias: float32 [2, 1024], P(None, 'tp'), may hold values from -3 to 3
Outputs:
- attended: bfloat16 [32768, 5120], P('ctx', 'tp')
Inputs may be any that keep to these rules, and one draw needn't show every extreme that they name: The 256 files fill the 32768 positions in order; their lengths sum to 32768 and the longest is exactly 2048.
All inputs are finite; a program needn't handle non-finite values.
Results may differ from a plain program's by a relative error of at most 0.006.
Values may be sent and summed in bfloat16 or wider, within the bound.
A program may use at most 128 MiB of HBM per device.

v0:
```python
import jax
import jax.numpy as jnp
from jax import lax
from jax.sharding import PartitionSpec as P

D = 5120
HD = 128
CYCLE = 4


def shifted(value, axis, steps):
    count = lax.axis_size(axis)
    leading, last = (max(0, -steps), min(count, count - steps))
    return lax.ppermute(value, axis, [(source, source + steps) for source in range(leading, last)])


def body(hidden, queries, lengths, norm_gain, kv_weight, kv_bias):
    tok = hidden.shape[0]
    xfull = hidden.astype(jnp.float32)
    squares = lax.psum(jnp.sum(xfull * xfull, axis=1), "tp")
    scale_rows = lax.rsqrt(squares / D + 1e-06)
    normed = (xfull * scale_rows[:, None] * norm_gain[None, :]).astype(jnp.bfloat16)
    flat_weight = kv_weight.reshape(kv_weight.shape[0], -1)
    summed = jnp.dot(
        lax.all_gather(normed, "tp", axis=1, tiled=True),
        flat_weight,
        preferred_element_type=jnp.float32,
    )
    kv_local = (
        (summed + kv_bias.reshape(-1)[None, :])
        .astype(jnp.bfloat16)
        .reshape(tok, 2, kv_weight.shape[2])
    )
    kv_heads = kv_weight.shape[2] // HD
    group = queries.shape[1] // HD // kv_heads
    qrows = queries.reshape(tok, kv_heads, group, HD)
    device = lax.axis_index("ctx")
    ends = jnp.cumsum(lengths)
    score_scale = HD ** (-0.5)

    def docs_of(first):
        positions = first + jnp.arange(tok, dtype=jnp.int32)
        found = jnp.sum((positions[:, None] >= ends[None, :]).astype(jnp.int32), axis=1)
        return (found, positions)

    qdoc, qpos = docs_of(device * tok)

    def attend(state, block, back):
        best, mass, acc = state
        kdoc, kpos = docs_of((device - back) * tok)
        kdoc = jnp.where(device - back >= 0, kdoc, -1)
        keys = block[:, 0].reshape(tok, kv_heads, HD)
        values = block[:, 1].reshape(tok, kv_heads, HD)
        scores = (
            jnp.einsum("qgjd,kgd->gjqk", qrows, keys, preferred_element_type=jnp.float32)
            * score_scale
        )
        visible = (qdoc[:, None] == kdoc[None, :]) & (kpos[None, :] <= qpos[:, None])
        scores = jnp.where(visible[None, None], scores, -1e30)
        top = jnp.maximum(best, jnp.max(scores, axis=-1))
        probs = jnp.exp(scores - top[..., None])
        shrink = jnp.exp(best - top)
        mass = mass * shrink + jnp.sum(probs, axis=-1)
        acc = acc * shrink[..., None] + jnp.einsum(
            "gjqk,kgd->gjqd", probs.astype(jnp.bfloat16), values, preferred_element_type=jnp.float32
        )
        return (top, mass, acc)

    state = (
        jnp.full((kv_heads, group, tok), -1e30, jnp.float32),
        jnp.zeros((kv_heads, group, tok), jnp.float32),
        jnp.zeros((kv_heads, group, tok, HD), jnp.float32),
    )
    state = attend(state, kv_local, 0)
    moving = kv_local
    for back in range(1, CYCLE + 1):
        moving = shifted(moving, "ctx", 1)
        state = attend(state, moving, back)
    best, mass, acc = state
    result = acc / mass[..., None]
    return result.transpose(2, 0, 1, 3).reshape(tok, queries.shape[1]).astype(jnp.bfloat16)


def solution(mesh):
    in_specs = (P("ctx", "tp"), P("ctx", "tp"), P(), P("tp"), P(None, None, "tp"), P(None, "tp"))
    out_specs = P("ctx", "tp")
    return jax.shard_map(body, mesh=mesh, in_specs=in_specs, out_specs=out_specs, check_vma=False)
```

profile of v0, /device:TPU:4, one launch (start us, length us, event | category | flops | bytes accessed | tf_op | source)
XLA Modules:
  0.0 223.8 jit_solution(11458401559064904060)
XLA Ops:
  6.5 1.8 fusion.30
  8.3 6.6 %psum.7 = f32[512]{0:T(512)S(1)} all-reduce(f32[512]{0:T(512)S(1)} %fusion.30), channel_id=1, replica_groups=mesh['ctx'=64,'tp'=4] {'tp'}, use_global_device_ids=true, to_apply=%region_4.5 | all-reduce | flops 512 | bytes 4096 | tf_op jit(solution)/shard_map/psum | solution.py:20
  14.9 2.7 %fusion.32 = bf16[512,1280]{1,0:T(8,128)(2,1)} fusion(bf16[512,1280]{1,0:T(8,128)(2,1)} %param.6, f32[1280]{0:T(1024)} %param.9, f32[512]{0:T(512)S(1)} %add_rsqrt_fusion), kind=kLoop, calls=%fused_computation.39 | loop fusion | flops 2621440 | bytes 2628608 | tf_op jit(solution)/shard_map/convert_element_type | solution.py:22
  17.6 0.0 all-gather.2.cloned.1.call-update
  17.7 1.0 reduce-window.9
  18.7 0.1 slice.37
  18.8 5.7 %copy.82 = bf16[640,8,2,256]{3,1,2,0:T(8,128)(2,1)} copy(bf16[640,8,2,256]{3,2,1,0:T(2,128)(2,1)} %bitcast.263) | data formatting | bytes 10485760
  24.5 0.6 copy.35
  25.2 0.1 slice_reduce_fusion
  25.3 0.1 add_bitcast_fusion
  25.4 0.9 convert_reduce_fusion
  26.4 1.4 compare_and_fusion.4
  27.8 49.7 %all-gather.2.cloned.1.call-done = bf16[512,5120]{1,0:T(8,128)(2,1)} async-done(((bf16[512,1280]{1,0:T(8,128)(2,1)}), bf16[512,5120]{1,0:T(8,128)(2,1)}) %all-gather.2.cloned.1.call-update) | async-done | bytes 5242896 | tf_op jit(solution)/shard_map/all_gather | solution.py:25
  77.5 7.0 %fusion.41 = bf16[512,512]{0,1:T(8,128)(2,1)S(1)} fusion(bf16[512,5120]{1,0:T(8,128)(2,1)} %all-gather.2.cloned.1.call-done, bf16[5120,512]{1,0:T(8,128)(2,1)} %bitcast.264, f32[512]{0:T(512)S(1)} %bitcast.279), kind=kOutput, calls=%fused_computation.52 | convolution fusion | flops 2684878848 | bytes 11012096 | tf_op jit(solution)/shard_map/dot_general | solution.py:24
  84.5 3.5 %collective-permute-start = (bf16[512,2,256]{0,2,1:T(8,128)(2,1)S(1)}, bf16[512,2,256]{0,2,1:T(8,128)(2,1)S(1)}, u32[]{:S(2)}, u32[]{:S(2)}) collective-permute-start(bf16[512,2,256]{0,2,1:T(8,128)(2,1)S(1)} %bitcast.271), channel_id=1, source_target_pairs={{0,4},{4,8},{8,12},{12,16},{16,20},{20,24},{24,28},{28,32},{32,36}... | collective-permute-start | bytes 1572872 | tf_op jit(solution)/shard_map/ppermute | solution.py:14
  88.0 0.7 fusion.65
  88.7 1.9 fusion.10
  90.6 16.3 %collective-permute-done = bf16[512,2,256]{0,2,1:T(8,128)(2,1)S(1)} collective-permute-done((bf16[512,2,256]{0,2,1:T(8,128)(2,1)S(1)}, bf16[512,2,256]{0,2,1:T(8,128)(2,1)S(1)}, u32[]{:S(2)}, u32[]{:S(2)}) %collective-permute-start) | collective-permute-done | bytes 524320 | tf_op jit(solution)/shard_map/ppermute | solution.py:14
  106.9 1.9 collective-permute-start.1
  108.8 0.7 fusion.66
  109.6 5.7 %fusion.11 = (f32[2,5,512]{2,1,0:T(8,128)S(1)}, f32[2,512,512,5]{2,1,3,0:T(8,128)}) fusion(pred[512,512]{0,1:T(8,128)(4,1)S(1)} %get-tuple-element.35, bf16[512,2,128,1]{0,2,3,1:T(8,128)(2,1)S(1)} %bitcast.268, bf16[512,2,5,128]{0,3,2,1:T(8,128)(2,1)S(1)} %bitcast.251), kind=kOutput, calls=%fused_computation.21 | convolution fusion | flops 678947840 | bytes 12341248 | tf_op jit(solution)/shard_map/qgjd,kgd->gjqk/dot_general | solution.py:55
  115.3 13.2 %collective-permute-done.1 = bf16[512,2,256]{0,2,1:T(8,128)(2,1)S(1)} collective-permute-done((bf16[512,2,256]{0,2,1:T(8,128)(2,1)S(1)}, bf16[512,2,256]{0,2,1:T(8,128)(2,1)S(1)}, u32[]{:S(2)}, u32[]{:S(2)}) %collective-permute-start.1) | collective-permute-done | bytes 524320 | tf_op jit(solution)/shard_map/ppermute | solution.py:14
  128.5 2.1 collective-permute-start.2
  130.6 0.8 fusion.67
  131.3 5.9 %fusion.12 = (f32[2,5,512]{2,1,0:T(8,128)S(1)}, f32[2,512,512,5]{2,1,3,0:T(8,128)}) fusion(pred[512,512]{0,1:T(8,128)(4,1)S(1)} %get-tuple-element.32, bf16[512,2,128,1]{0,2,3,1:T(8,128)(2,1)S(1)} %bitcast.269, bf16[512,2,5,128]{0,3,2,1:T(8,128)(2,1)S(1)} %bitcast.252), kind=kOutput, calls=%fused_computation.22 | convolution fusion | flops 678947840 | bytes 12341248 | tf_op jit(solution)/shard_map/qgjd,kgd->gjqk/dot_general | solution.py:55
  137.2 12.0 %collective-permute-done.2 = bf16[512,2,256]{0,2,1:T(8,128)(2,1)S(1)} collective-permute-done((bf16[512,2,256]{0,2,1:T(8,128)(2,1)S(1)}, bf16[512,2,256]{0,2,1:T(8,128)(2,1)S(1)}, u32[]{:S(2)}, u32[]{:S(2)}) %collective-permute-start.2) | collective-permute-done | bytes 524320 | tf_op jit(solution)/shard_map/ppermute | solution.py:14
  149.2 1.9 collective-permute-start.3
  151.1 0.7 fusion.68
  151.8 5.9 %fusion.13 = (f32[2,5,512]{2,1,0:T(8,128)S(1)}, f32[2,512,512,5]{2,1,3,0:T(8,128)}) fusion(pred[512,512]{0,1:T(8,128)(4,1)S(1)} %get-tuple-element.33, bf16[512,2,128,1]{0,2,3,1:T(8,128)(2,1)S(1)} %bitcast.270, bf16[512,2,5,128]{0,3,2,1:T(8,128)(2,1)S(1)} %bitcast.253), kind=kOutput, calls=%fused_computation.23 | convolution fusion | flops 678947840 | bytes 12341248 | tf_op jit(solution)/shard_map/qgjd,kgd->gjqk/dot_general | solution.py:55
  157.7 11.3 %collective-permute-done.3 = bf16[512,2,256]{0,2,1:T(8,128)(2,1)S(1)} collective-permute-done((bf16[512,2,256]{0,2,1:T(8,128)(2,1)S(1)}, bf16[512,2,256]{0,2,1:T(8,128)(2,1)S(1)}, u32[]{:S(2)}, u32[]{:S(2)}) %collective-permute-start.3) | collective-permute-done | bytes 524320 | tf_op jit(solution)/shard_map/ppermute | solution.py:14
  169.0 0.7 fusion.64
  169.7 5.7 %fusion.14 = (f32[2,5,512]{2,1,0:T(8,128)S(1)}, f32[2,512,512,5]{2,1,3,0:T(8,128)}) fusion(pred[512,512]{0,1:T(8,128)(4,1)S(1)} %get-tuple-element.34, bf16[512,2,128,1]{0,2,3,1:T(8,128)(2,1)S(1)} %bitcast.266, bf16[512,2,5,128]{0,3,2,1:T(8,128)(2,1)S(1)} %bitcast.254), kind=kOutput, calls=%fused_computation.24 | convolution fusion | flops 678947840 | bytes 12341248 | tf_op jit(solution)/shard_map/qgjd,kgd->gjqk/dot_general | solution.py:55
  175.4 0.6 fusion.62
  176.1 2.2 fusion
  178.3 0.0 slice-start.2
  178.3 5.7 %fusion.23 = f32[2,5,512,128]{2,3,1,0:T(8,128)} fusion(bf16[512,2,128,1]{0,2,3,1:T(8,128)(2,1)} %bitcast.273, f32[2,512,512,5]{2,1,3,0:T(8,128)S(1)} %get-tuple-element.45, f32[2,5,512]{2,1,0:T(8,128)S(1)} %get-tuple-element.30, pred[512,512]{0,1:T(8,128)(4,1)S(1)} %get-tuple-element.31), kind=kOutput, calls=%fused_computation.29 | convolution fusion | flops 681574400 | bytes 13651968 | tf_op jit(solution)/shard_map/gjqk,kgd->gjqd/dot_general | solution.py:64
  184.0 0.0 slice-start.6
  184.0 0.0 slice-start.7
  184.0 3.0 %fusion.2 = f32[2,5,512]{2,1,0:T(8,128)S(1)} fusion(f32[2,512,512,5]{2,1,3,0:T(8,128)S(1)} %bitcast.256, f32[2,5,512]{2,1,0:T(8,128)} %get-tuple-element.17, pred[512,512]{0,1:T(8,128)(4,1)S(1)} %get-tuple-element.35), kind=kLoop, calls=%fused_computation.12 | loop fusion | flops 10480640 | bytes 10788864 | tf_op jit(solution)/shard_map/reduce_sum | solution.py:63
  187.1 0.0 slice-start.8
  187.1 5.0 %fusion.21 = f32[2,5,512,128]{2,3,1,0:T(8,128)} fusion(bf16[512,2,128,1]{0,2,3,1:T(8,128)(2,1)S(1)} %bitcast.275, f32[2,512,512,5]{2,1,3,0:T(8,128)S(1)} %bitcast.256, f32[2,5,512]{2,1,0:T(8,128)} %get-tuple-element.17, pred[512,512]{0,1:T(8,128)(4,1)S(1)} %get-tuple-element.35), kind=kOutput, calls=%fused_computation.28 | convolution fusion | flops 681574400 | bytes 13651968 | tf_op jit(solution)/shard_map/gjqk,kgd->gjqd/dot_general | solution.py:64
  192.1 0.0 slice-done.7
  192.1 0.0 slice-done.8
  192.1 0.0 slice-start.9
  192.1 0.0 slice-start.10
  192.1 3.6 %fusion.4 = f32[2,5,512]{2,1,0:T(8,128)} fusion(f32[2,512,512,5]{2,1,3,0:T(8,128)S(1)} %bitcast.260, f32[2,5,512]{2,1,0:T(8,128)} %get-tuple-element.16, pred[512,512]{0,1:T(8,128)(4,1)S(1)} %get-tuple-element.32), kind=kLoop, calls=%fused_computation.14 | loop fusion | flops 10480640 | bytes 10788864 | tf_op jit(solution)/shard_map/reduce_sum | solution.py:63
  195.8 5.0 %fusion.19 = f32[2,5,512,128]{2,3,1,0:T(8,128)} fusion(bf16[512,2,128,1]{0,2,3,1:T(8,128)(2,1)S(1)} %bitcast.276, f32[2,512,512,5]{2,1,3,0:T(8,128)S(1)} %bitcast.260, f32[2,5,512]{2,1,0:T(8,128)} %get-tuple-element.16, pred[512,512]{0,1:T(8,128)(4,1)S(1)} %get-tuple-element.32), kind=kOutput, calls=%fused_computation.27 | convolution fusion | flops 681574400 | bytes 13651968 | tf_op jit(solution)/shard_map/gjqk,kgd->gjqd/dot_general | solution.py:64
  200.8 0.0 slice-done.9
  200.8 0.0 slice-done.11
  200.8 0.0 slice-start.3
  200.8 0.0 slice-start.4
  200.8 2.2 fusion.6
  203.0 0.0 slice-start.5
  203.0 0.0 copy-start.5
  203.0 0.0 copy-start.1
  203.0 4.0 %fusion.17 = f32[2,5,512,128]{2,3,1,0:T(8,128)} fusion(bf16[512,2,128,1]{0,2,3,1:T(8,128)(2,1)S(1)} %bitcast.277, f32[2,512,512,5]{2,1,3,0:T(8,128)S(1)} %bitcast.262, f32[2,5,512]{2,1,0:T(8,128)S(1)} %get-tuple-element.15, pred[512,512]{0,1:T(8,128)(4,1)S(1)} %get-tuple-element.33), kind=kOutput, calls=%fused_computation.26 | convolution fusion | flops 681574400 | bytes 13651968 | tf_op jit(solution)/shard_map/gjqk,kgd->gjqd/dot_general | solution.py:64
  207.1 0.0 slice-done.3
  207.1 0.0 slice-done.4
  207.1 0.0 slice-done.5
  207.1 2.2 fusion.8
  209.4 0.2 copy-done.8
  209.6 0.8 copy-done.9
  210.4 5.1 %fusion.34 = bf16[512,2,5,128]{0,3,2,1:T(8,128)(2,1)S(1)} fusion(f32[2,5,512,128]{2,3,1,0:T(8,128)} %fusion.17, f32[2,5,512,128]{2,3,1,0:T(8,128)S(1)} %copy-done.9, f32[2,5,512,128]{2,3,1,0:T(8,128)S(1)} %copy-done.8, f32[2,5,512,128]{2,3,1,0:T(8,128)S(1)} %copy-done.7, bf16[512,2,128,1]{0,2,3,1:T(8,128)(2,1)S(1)} %bitcast.274, ...), kind=kOutput, calls=%fused_computation.42 | convolution fusion | flops 688783360 | bytes 22949888 | tf_op jit(solution)/shard_map/gjqk,kgd->gjqd/dot_general | solution.py:64
  215.5 1.4 copy.51
  (41 shorter events, 0.2 us)
Async XLA Ops:
  6.5 18.0 %copy-start.6 = (f32[2,256]{1,0:T(2,128)S(1)}, f32[2,256]{1,0:T(2,128)}, u32[]{:S(2)}) copy-start(f32[2,256]{1,0:T(2,128)} %param.11) | copy-start | bytes 6148
  6.5 18.0 %copy-start = (bf16[512,1280]{1,0:T(8,128)(2,1)S(1)}, bf16[512,1280]{1,0:T(8,128)(2,1)}, u32[]{:S(2)}) copy-start(bf16[512,1280]{1,0:T(8,128)(2,1)} %param.7) | copy-start | bytes 3932164
  6.5 71.0 %all-gather.2.cloned.1.call-start = ((), (), s32[]{:S(2)}) async-start(), calls=%async_computation | async-start | bytes 6553600 | tf_op jit(solution)/shard_map/all_gather | solution.py:25
  84.5 22.4 %collective-permute-start = (bf16[512,2,256]{0,2,1:T(8,128)(2,1)S(1)}, bf16[512,2,256]{0,2,1:T(8,128)(2,1)S(1)}, u32[]{:S(2)}, u32[]{:S(2)}) collective-permute-start(bf16[512,2,256]{0,2,1:T(8,128)(2,1)S(1)} %bitcast.271), channel_id=1, source_target_pairs={{0,4},{4,8},{8,12},{12,16},{16,20},{20,24},{24,28},{28,32},{32,36}... | collective-permute-start | bytes 1572872 | tf_op jit(solution)/shard_map/ppermute | solution.py:14
  106.9 21.5 %collective-permute-start.1 = (bf16[512,2,256]{0,2,1:T(8,128)(2,1)S(1)}, bf16[512,2,256]{0,2,1:T(8,128)(2,1)S(1)}, u32[]{:S(2)}, u32[]{:S(2)}) collective-permute-start(bf16[512,2,256]{0,2,1:T(8,128)(2,1)S(1)} %collective-permute-done), channel_id=1, source_target_pairs={{0,4},{4,8},{8,12},{12,16},{16,20},{20,24},{24,28},{28,32},{32,36}... | collective-permute-start | bytes 1572872 | tf_op jit(solution)/shard_map/ppermute | solution.py:14
  128.5 20.7 %collective-permute-start.2 = (bf16[512,2,256]{0,2,1:T(8,128)(2,1)S(1)}, bf16[512,2,256]{0,2,1:T(8,128)(2,1)S(1)}, u32[]{:S(2)}, u32[]{:S(2)}) collective-permute-start(bf16[512,2,256]{0,2,1:T(8,128)(2,1)S(1)} %collective-permute-done.1), channel_id=1, source_target_pairs={{0,4},{4,8},{8,12},{12,16},{16,20},{20,24},{24,28},{28,32},{32,36}... | collective-permute-start | bytes 1572872 | tf_op jit(solution)/shard_map/ppermute | solution.py:14
  149.2 19.8 %collective-permute-start.3 = (bf16[512,2,256]{0,2,1:T(8,128)(2,1)S(1)}, bf16[512,2,256]{0,2,1:T(8,128)(2,1)S(1)}, u32[]{:S(2)}, u32[]{:S(2)}) collective-permute-start(bf16[512,2,256]{0,2,1:T(8,128)(2,1)S(1)} %collective-permute-done.2), channel_id=1, source_target_pairs={{0,4},{4,8},{8,12},{12,16},{16,20},{20,24},{24,28},{28,32},{32,36}... | collective-permute-start | bytes 1572872 | tf_op jit(solution)/shard_map/ppermute | solution.py:14
  176.1 7.9 %slice-start = ((s8[10485760]{0:T(1024)(128)(4,1)}), s8[4194304]{0:T(1024)(128)(4,1)S(1)}, s32[]{:S(2)}) async-start(s8[10485760]{0:T(1024)(128)(4,1)} %bitcast.255), calls=%async_computation.1 | async-start | bytes 8388608
  176.1 7.9 %slice-start.1 = ((s8[10485760]{0:T(1024)(128)(4,1)}), s8[4194304]{0:T(1024)(128)(4,1)S(1)}, s32[]{:S(2)}) async-start(s8[10485760]{0:T(1024)(128)(4,1)} %bitcast.255), calls=%async_computation.2 | async-start | bytes 8388608
  178.3 5.7 %slice-start.2 = ((s8[10485760]{0:T(1024)(128)(4,1)}), s8[2097152]{0:T(1024)(128)(4,1)S(1)}, s32[]{:S(2)}) async-start(s8[10485760]{0:T(1024)(128)(4,1)} %bitcast.255), calls=%async_computation.3 | async-start | bytes 4194304
  183.9 3.1 %copy-start.2 = (bf16[512,1,256]{0,2,1:T(8,128)(2,1)S(1)}, bf16[512,1,256]{0,2,1:T(8,128)(2,1)}, u32[]{:S(2)}) copy-start(bf16[512,1,256]{0,2,1:T(8,128)(2,1)} %get-tuple-element.22) | copy-start | bytes 786436
  184.0 8.1 %slice-start.6 = ((s8[10485760]{0:T(1024)(128)(4,1)}), s8[4194304]{0:T(1024)(128)(4,1)S(1)}, s32[]{:S(2)}) async-start(s8[10485760]{0:T(1024)(128)(4,1)} %bitcast.259), calls=%async_computation.7 | async-start | bytes 8388608
  184.0 8.1 %slice-start.7 = ((s8[10485760]{0:T(1024)(128)(4,1)}), s8[4194304]{0:T(1024)(128)(4,1)S(1)}, s32[]{:S(2)}) async-start(s8[10485760]{0:T(1024)(128)(4,1)} %bitcast.259), calls=%async_computation.8 | async-start | bytes 8388608
  187.1 5.0 %slice-start.8 = ((s8[10485760]{0:T(1024)(128)(4,1)}), s8[2097152]{0:T(1024)(128)(4,1)S(1)}, s32[]{:S(2)}) async-start(s8[10485760]{0:T(1024)(128)(4,1)} %bitcast.259), calls=%async_computation.9 | async-start | bytes 4194304
  192.1 3.7 %copy-start.3 = (bf16[512,1,256]{0,2,1:T(8,128)(2,1)S(1)}, bf16[512,1,256]{0,2,1:T(8,128)(2,1)}, u32[]{:S(2)}) copy-start(bf16[512,1,256]{0,2,1:T(8,128)(2,1)} %get-tuple-element.24) | copy-start | bytes 786436
  192.1 8.7 %slice-start.9 = ((s8[10485760]{0:T(1024)(128)(4,1)}), s8[4194304]{0:T(1024)(128)(4,1)S(1)}, s32[]{:S(2)}) async-start(s8[10485760]{0:T(1024)(128)(4,1)} %bitcast.261), calls=%async_computation.10 | async-start | bytes 8388608
  192.1 8.7 %slice-start.10 = ((s8[10485760]{0:T(1024)(128)(4,1)}), s8[4194304]{0:T(1024)(128)(4,1)S(1)}, s32[]{:S(2)}) async-start(s8[10485760]{0:T(1024)(128)(4,1)} %bitcast.261), calls=%async_computation.11 | async-start | bytes 8388608
  195.8 5.0 %slice-start.11 = ((s8[10485760]{0:T(1024)(128)(4,1)}), s8[2097152]{0:T(1024)(128)(4,1)S(1)}, s32[]{:S(2)}) async-start(s8[10485760]{0:T(1024)(128)(4,1)} %bitcast.261), calls=%async_computation.12 | async-start | bytes 4194304
  195.8 7.2 %copy-start.4 = (bf16[512,1,256]{0,2,1:T(8,128)(2,1)S(1)}, bf16[512,1,256]{0,2,1:T(8,128)(2,1)}, u32[]{:S(2)}) copy-start(bf16[512,1,256]{0,2,1:T(8,128)(2,1)} %get-tuple-element.27) | copy-start | bytes 786436
  200.8 6.3 %slice-start.3 = ((s8[10485760]{0:T(1024)(128)(4,1)}), s8[4194304]{0:T(1024)(128)(4,1)S(1)}, s32[]{:S(2)}) async-start(s8[10485760]{0:T(1024)(128)(4,1)} %bitcast.257), calls=%async_computation.4 | async-start | bytes 8388608
  200.8 6.3 %slice-start.4 = ((s8[10485760]{0:T(1024)(128)(4,1)}), s8[4194304]{0:T(1024)(128)(4,1)S(1)}, s32[]{:S(2)}) async-start(s8[10485760]{0:T(1024)(128)(4,1)} %bitcast.257), calls=%async_computation.5 | async-start | bytes 8388608
  203.0 4.1 %slice-start.5 = ((s8[10485760]{0:T(1024)(128)(4,1)}), s8[2097152]{0:T(1024)(128)(4,1)S(1)}, s32[]{:S(2)}) async-start(s8[10485760]{0:T(1024)(128)(4,1)} %bitcast.257), calls=%async_computation.6 | async-start | bytes 4194304
  203.0 6.3 %copy-start.5 = (f32[2,5,512]{2,1,0:T(8,128)S(1)}, f32[2,5,512]{2,1,0:T(8,128)}, u32[]{:S(2)}) copy-start(f32[2,5,512]{2,1,0:T(8,128)} %fusion.4) | copy-start | bytes 61444
  203.0 6.4 %copy-start.1 = (bf16[512,1,256]{0,2,1:T(8,128)(2,1)S(1)}, bf16[512,1,256]{0,2,1:T(8,128)(2,1)}, u32[]{:S(2)}) copy-start(bf16[512,1,256]{0,2,1:T(8,128)(2,1)} %get-tuple-element.18) | copy-start | bytes 786436
  207.1 2.3 %copy-start.7 = (f32[2,5,512,128]{2,3,1,0:T(8,128)S(1)}, f32[2,5,512,128]{2,3,1,0:T(8,128)}, u32[]{:S(2)}) copy-start(f32[2,5,512,128]{2,3,1,0:T(8,128)} %fusion.23) | copy-start | bytes 7864324
  207.1 2.5 %copy-start.8 = (f32[2,5,512,128]{2,3,1,0:T(8,128)S(1)}, f32[2,5,512,128]{2,3,1,0:T(8,128)}, u32[]{:S(2)}) copy-start(f32[2,5,512,128]{2,3,1,0:T(8,128)} %fusion.21) | copy-start | bytes 7864324
  207.1 3.3 %copy-start.9 = (f32[2,5,512,128]{2,3,1,0:T(8,128)S(1)}, f32[2,5,512,128]{2,3,1,0:T(8,128)}, u32[]{:S(2)}) copy-start(f32[2,5,512,128]{2,3,1,0:T(8,128)} %fusion.19) | copy-start | bytes 7864324
Sparse Core Ops, SparseCore 0:
  17.8 59.6 all-gather.1
where the time goes:
time: 224 us
  waiting for transfers between devices  102 us (46%)
  matrix products  56.9 us (25%)
  other arithmetic  21.9 us (10%)
  between operations  13.8 us (6%)
  local copies, waits for them, and re-layouts  12.8 us (6%)
  starting transfers between devices  9.37 us (4%)
  blocking collectives  6.6 us (3%)
    ppermute x4, waiting for transfers between devices, shifted(): lax.ppermute(value, axis, [(source, source + steps) for source in range(l...  52.7 us
    all_gather x1, waiting for transfers between devices, body(): lax.all_gather(normed, 'tp', axis=1, tiled=True)  49.7 us
    dot_general x5, matrix products, attend(): jnp.einsum('qgjd,kgd->gjqk', qrows, keys, preferred_element_type=jnp.floa...  25.1 us
    dot_general x5, matrix products, attend(): jnp.einsum('gjqk,kgd->gjqd', probs.astype(jnp.bfloat16), values, preferre...  24.8 us
    reduce_sum x5, other arithmetic, attend(): mass = mass * shrink + jnp.sum(probs, axis=-1)  13.2 us
    ppermute x4, starting transfers between devices, shifted(): lax.ppermute(value, axis, [(source, source + steps) for source in range(l...  9.37 us
    unnamed x47, local copies, waits for them, and re-layouts  7.45 us
    dot_general x1, matrix products, body(): jnp.dot(lax.all_gather(normed, 'tp', axis=1, tiled=True), flat_weight, pr...  6.97 us
  transfers between devices with their start and end apart: 5, of which 5 were waited for; matrix products, arithmetic and copies ran while one was open for 14% of the time, Pallas kernels for 0%

commit v1 on v0

--- a/solution.py
+++ b/solution.py
@@ -17,7 +17,9 @@
 def body(hidden, queries, lengths, norm_gain, kv_weight, kv_bias):
     tok = hidden.shape[0]
     xfull = hidden.astype(jnp.float32)
-    squares = lax.psum(jnp.sum(xfull * xfull, axis=1), "tp")
+    x_local = jnp.sum(xfull * xfull, axis=1)
+    taken_in = jax.lax.all_gather(x_local, "tp")
+    squares = jnp.sum(taken_in, 0)
     scale_rows = lax.rsqrt(squares / D + 1e-06)
     normed = (xfull * scale_rows[:, None] * norm_gain[None, :]).astype(jnp.bfloat16)
     flat_weight = kv_weight.reshape(kv_weight.shape[0], -1)

time: 224 us -> 223 us (level)
    psum x1 -> x0, blocking collectives: 6.6 us -> none  [body(): squares = lax.psum(jnp.sum(xfull * xfull, axis=1), 'tp')]
    all_gather x0 -> x1, blocking collectives: none -> 5.16 us  [body(): taken_in = jax.lax.all_gather(x_local, 'tp')]
  transfers between devices with their start and end apart: 5 -> 5, of which waited for: 5 -> 5; matrix products, arithmetic and copies ran while one was open for 14% -> 15% of each run, Pallas kernels for 0% -> 0%
where the time goes in v1:
time: 223 us; the launch traced here: 222 us
  waiting for transfers between devices  103 us (46%)
  matrix products  56.9 us (26%)
  other arithmetic  21.9 us (10%)
  between operations  13.8 us (6%)
  local copies, waits for them, and re-layouts  12.8 us (6%)
  starting transfers between devices  9.37 us (4%)
  blocking collectives  5.16 us (2%)
    ppermute x4, waiting for transfers between devices, shifted(): lax.ppermute(value, axis, [(source, source + steps) for source in range(l...  52.7 us
    all_gather x1, waiting for transfers between devices, body(): lax.all_gather(normed, 'tp', axis=1, tiled=True)  49.8 us
    dot_general x5, matrix products, attend(): jnp.einsum('qgjd,kgd->gjqk', qrows, keys, preferred_element_type=jnp.floa...  25.1 us
    dot_general x5, matrix products, attend(): jnp.einsum('gjqk,kgd->gjqd', probs.astype(jnp.bfloat16), values, preferre...  24.8 us
    reduce_sum x5, other arithmetic, attend(): mass = mass * shrink + jnp.sum(probs, axis=-1)  13.2 us
    ppermute x4, starting transfers between devices, shifted(): lax.ppermute(value, axis, [(source, source + steps) for source in range(l...  9.37 us
    unnamed x47, local copies, waits for them, and re-layouts  7.45 us
    dot_general x1, matrix products, body(): jnp.dot(lax.all_gather(normed, 'tp', axis=1, tiled=True), flat_weight, pr...  6.97 us
  transfers between devices with their start and end apart: 5, of which 5 were waited for; matrix products, arithmetic and copies ran while one was open for 15% of the time, Pallas kernels for 0%

profile of v1, /device:TPU:4, one launch (start us, length us, event | category | flops | bytes accessed | tf_op | source)
XLA Modules:
  0.0 222.4 jit_solution(2185084256315874108)
XLA Ops:
  6.5 0.0 all-gather.4.cloned.1.call-start
  6.5 1.8 fusion.30
  8.3 5.2 %all-gather.1 = f32[4,1,512]{2,1,0:T(1,128)S(1)} all-gather(f32[1,1,512]{2,1,0:T(1,128)S(1)} %bitcast.279), channel_id=2, replica_groups=mesh['ctx'=64,'tp'=4] {'tp'}, dimensions={0}, use_global_device_ids=true | all-gather | bytes 10240 | tf_op jit(solution)/shard_map/all_gather | solution.py:21
  13.5 2.7 %fusion.32 = bf16[512,1280]{1,0:T(8,128)(2,1)} fusion(bf16[512,1280]{1,0:T(8,128)(2,1)} %param.6, f32[1280]{0:T(1024)} %param.9, f32[512]{0:T(512)S(1)} %add_rsqrt_fusion), kind=kLoop, calls=%fused_computation.39 | loop fusion | flops 2621440 | bytes 2628608 | tf_op jit(solution)/shard_map/convert_element_type | solution.py:24
  16.2 0.0 all-gather.4.cloned.1.call-update
  16.3 1.0 reduce-window.9
  17.3 0.1 slice.37
  17.4 5.7 %copy.99 = bf16[640,8,2,256]{3,1,2,0:T(8,128)(2,1)} copy(bf16[640,8,2,256]{3,2,1,0:T(2,128)(2,1)} %bitcast.264) | data formatting | bytes 10485760
  23.1 0.0 copy-done.6
  23.1 0.0 copy-done
  23.1 0.6 copy.52
  23.8 0.1 slice_reduce_fusion
  23.9 0.1 add_bitcast_fusion
  24.0 0.9 convert_reduce_fusion
  25.0 1.4 compare_and_fusion.4
  26.4 49.8 %all-gather.4.cloned.1.call-done = bf16[512,5120]{1,0:T(8,128)(2,1)} async-done(((bf16[512,1280]{1,0:T(8,128)(2,1)}), bf16[512,5120]{1,0:T(8,128)(2,1)}) %all-gather.4.cloned.1.call-update) | async-done | bytes 5242896 | tf_op jit(solution)/shard_map/all_gather | solution.py:27
  76.2 7.0 %fusion.41 = bf16[512,512]{0,1:T(8,128)(2,1)S(1)} fusion(bf16[512,5120]{1,0:T(8,128)(2,1)} %all-gather.4.cloned.1.call-done, bf16[5120,512]{1,0:T(8,128)(2,1)} %bitcast.265, f32[512]{0:T(512)S(1)} %bitcast.281), kind=kOutput, calls=%fused_computation.52 | convolution fusion | flops 2684878848 | bytes 11012096 | tf_op jit(solution)/shard_map/dot_general | solution.py:26
  83.1 3.5 %collective-permute-start = (bf16[512,2,256]{0,2,1:T(8,128)(2,1)S(1)}, bf16[512,2,256]{0,2,1:T(8,128)(2,1)S(1)}, u32[]{:S(2)}, u32[]{:S(2)}) collective-permute-start(bf16[512,2,256]{0,2,1:T(8,128)(2,1)S(1)} %bitcast.272), channel_id=1, source_target_pairs={{0,4},{4,8},{8,12},{12,16},{16,20},{20,24},{24,28},{28,32},{32,36}... | collective-permute-start | bytes 1572872 | tf_op jit(solution)/shard_map/ppermute | solution.py:14
  86.6 0.7 fusion.65
  87.3 1.9 fusion.10
  89.3 16.3 %collective-permute-done = bf16[512,2,256]{0,2,1:T(8,128)(2,1)S(1)} collective-permute-done((bf16[512,2,256]{0,2,1:T(8,128)(2,1)S(1)}, bf16[512,2,256]{0,2,1:T(8,128)(2,1)S(1)}, u32[]{:S(2)}, u32[]{:S(2)}) %collective-permute-start) | collective-permute-done | bytes 524320 | tf_op jit(solution)/shard_map/ppermute | solution.py:14
  105.5 1.9 collective-permute-start.1
  107.5 0.7 fusion.66
  108.2 5.7 %fusion.11 = (f32[2,5,512]{2,1,0:T(8,128)S(1)}, f32[2,512,512,5]{2,1,3,0:T(8,128)}) fusion(pred[512,512]{0,1:T(8,128)(4,1)S(1)} %get-tuple-element.35, bf16[512,2,128,1]{0,2,3,1:T(8,128)(2,1)S(1)} %bitcast.269, bf16[512,2,5,128]{0,3,2,1:T(8,128)(2,1)S(1)} %bitcast.252), kind=kOutput, calls=%fused_computation.21 | convolution fusion | flops 678947840 | bytes 12341248 | tf_op jit(solution)/shard_map/qgjd,kgd->gjqk/dot_general | solution.py:57
  113.9 13.2 %collective-permute-done.1 = bf16[512,2,256]{0,2,1:T(8,128)(2,1)S(1)} collective-permute-done((bf16[512,2,256]{0,2,1:T(8,128)(2,1)S(1)}, bf16[512,2,256]{0,2,1:T(8,128)(2,1)S(1)}, u32[]{:S(2)}, u32[]{:S(2)}) %collective-permute-start.1) | collective-permute-done | bytes 524320 | tf_op jit(solution)/shard_map/ppermute | solution.py:14
  127.1 2.1 collective-permute-start.2
  129.2 0.8 fusion.67
  129.9 5.9 %fusion.12 = (f32[2,5,512]{2,1,0:T(8,128)S(1)}, f32[2,512,512,5]{2,1,3,0:T(8,128)}) fusion(pred[512,512]{0,1:T(8,128)(4,1)S(1)} %get-tuple-element.32, bf16[512,2,128,1]{0,2,3,1:T(8,128)(2,1)S(1)} %bitcast.270, bf16[512,2,5,128]{0,3,2,1:T(8,128)(2,1)S(1)} %bitcast.253), kind=kOutput, calls=%fused_computation.22 | convolution fusion | flops 678947840 | bytes 12341248 | tf_op jit(solution)/shard_map/qgjd,kgd->gjqk/dot_general | solution.py:57
  135.8 12.0 %collective-permute-done.2 = bf16[512,2,256]{0,2,1:T(8,128)(2,1)S(1)} collective-permute-done((bf16[512,2,256]{0,2,1:T(8,128)(2,1)S(1)}, bf16[512,2,256]{0,2,1:T(8,128)(2,1)S(1)}, u32[]{:S(2)}, u32[]{:S(2)}) %collective-permute-start.2) | collective-permute-done | bytes 524320 | tf_op jit(solution)/shard_map/ppermute | solution.py:14
  147.8 1.9 collective-permute-start.3
  149.7 0.7 fusion.68
  150.5 5.9 %fusion.13 = (f32[2,5,512]{2,1,0:T(8,128)S(1)}, f32[2,512,512,5]{2,1,3,0:T(8,128)}) fusion(pred[512,512]{0,1:T(8,128)(4,1)S(1)} %get-tuple-element.33, bf16[512,2,128,1]{0,2,3,1:T(8,128)(2,1)S(1)} %bitcast.271, bf16[512,2,5,128]{0,3,2,1:T(8,128)(2,1)S(1)} %bitcast.254), kind=kOutput, calls=%fused_computation.23 | convolution fusion | flops 678947840 | bytes 12341248 | tf_op jit(solution)/shard_map/qgjd,kgd->gjqk/dot_general | solution.py:57
  156.4 11.3 %collective-permute-done.3 = bf16[512,2,256]{0,2,1:T(8,128)(2,1)S(1)} collective-permute-done((bf16[512,2,256]{0,2,1:T(8,128)(2,1)S(1)}, bf16[512,2,256]{0,2,1:T(8,128)(2,1)S(1)}, u32[]{:S(2)}, u32[]{:S(2)}) %collective-permute-start.3) | collective-permute-done | bytes 524320 | tf_op jit(solution)/shard_map/ppermute | solution.py:14
  167.6 0.7 fusion.64
  168.3 5.7 %fusion.14 = (f32[2,5,512]{2,1,0:T(8,128)S(1)}, f32[2,512,512,5]{2,1,3,0:T(8,128)}) fusion(pred[512,512]{0,1:T(8,128)(4,1)S(1)} %get-tuple-element.34, bf16[512,2,128,1]{0,2,3,1:T(8,128)(2,1)S(1)} %bitcast.267, bf16[512,2,5,128]{0,3,2,1:T(8,128)(2,1)S(1)} %bitcast.255), kind=kOutput, calls=%fused_computation.24 | convolution fusion | flops 678947840 | bytes 12341248 | tf_op jit(solution)/shard_map/qgjd,kgd->gjqk/dot_general | solution.py:57
  174.1 0.6 fusion.62
  174.7 2.2 fusion
  176.9 0.0 slice-start.2
  176.9 5.7 %fusion.23 = f32[2,5,512,128]{2,3,1,0:T(8,128)} fusion(bf16[512,2,128,1]{0,2,3,1:T(8,128)(2,1)} %bitcast.274, f32[2,512,512,5]{2,1,3,0:T(8,128)S(1)} %get-tuple-element.45, f32[2,5,512]{2,1,0:T(8,128)S(1)} %get-tuple-element.30, pred[512,512]{0,1:T(8,128)(4,1)S(1)} %get-tuple-element.31), kind=kOutput, calls=%fused_computation.29 | convolution fusion | flops 681574400 | bytes 13651968 | tf_op jit(solution)/shard_map/gjqk,kgd->gjqd/dot_general | solution.py:66
  182.6 0.0 slice-done
  182.6 0.0 slice-done.1
  182.6 0.0 slice-done.2
  182.6 0.0 slice-start.6
  182.6 0.0 slice-start.7
  182.6 3.0 %fusion.2 = f32[2,5,512]{2,1,0:T(8,128)S(1)} fusion(f32[2,512,512,5]{2,1,3,0:T(8,128)S(1)} %bitcast.257, f32[2,5,512]{2,1,0:T(8,128)} %get-tuple-element.17, pred[512,512]{0,1:T(8,128)(4,1)S(1)} %get-tuple-element.35), kind=kLoop, calls=%fused_computation.12 | loop fusion | flops 10480640 | bytes 10788864 | tf_op jit(solution)/shard_map/reduce_sum | solution.py:65
  185.7 0.0 copy-done.2
  185.7 0.0 slice-start.8
  185.7 5.0 %fusion.21 = f32[2,5,512,128]{2,3,1,0:T(8,128)} fusion(bf16[512,2,128,1]{0,2,3,1:T(8,128)(2,1)S(1)} %bitcast.276, f32[2,512,512,5]{2,1,3,0:T(8,128)S(1)} %bitcast.257, f32[2,5,512]{2,1,0:T(8,128)} %get-tuple-element.17, pred[512,512]{0,1:T(8,128)(4,1)S(1)} %get-tuple-element.35), kind=kOutput, calls=%fused_computation.28 | convolution fusion | flops 681574400 | bytes 13651968 | tf_op jit(solution)/shard_map/gjqk,kgd->gjqd/dot_general | solution.py:66
  190.7 0.0 slice-start.9
  190.7 0.0 slice-start.10
  190.8 3.6 %fusion.4 = f32[2,5,512]{2,1,0:T(8,128)} fusion(f32[2,512,512,5]{2,1,3,0:T(8,128)S(1)} %bitcast.261, f32[2,5,512]{2,1,0:T(8,128)} %get-tuple-element.16, pred[512,512]{0,1:T(8,128)(4,1)S(1)} %get-tuple-element.32), kind=kLoop, calls=%fused_computation.14 | loop fusion | flops 10480640 | bytes 10788864 | tf_op jit(solution)/shard_map/reduce_sum | solution.py:65
  194.4 5.0 %fusion.19 = f32[2,5,512,128]{2,3,1,0:T(8,128)} fusion(bf16[512,2,128,1]{0,2,3,1:T(8,128)(2,1)S(1)} %bitcast.277, f32[2,512,512,5]{2,1,3,0:T(8,128)S(1)} %bitcast.261, f32[2,5,512]{2,1,0:T(8,128)} %get-tuple-element.16, pred[512,512]{0,1:T(8,128)(4,1)S(1)} %get-tuple-element.32), kind=kOutput, calls=%fused_computation.27 | convolution fusion | flops 681574400 | bytes 13651968 | tf_op jit(solution)/shard_map/gjqk,kgd->gjqd/dot_general | solution.py:66
  199.4 0.0 slice-done.10
  199.4 0.0 slice-start.3
  199.4 0.0 slice-start.4
  199.4 2.2 fusion.6
  201.6 0.0 copy-done.4
  201.6 0.0 slice-start.5
  201.7 4.0 %fusion.17 = f32[2,5,512,128]{2,3,1,0:T(8,128)} fusion(bf16[512,2,128,1]{0,2,3,1:T(8,128)(2,1)S(1)} %bitcast.278, f32[2,512,512,5]{2,1,3,0:T(8,128)S(1)} %bitcast.263, f32[2,5,512]{2,1,0:T(8,128)S(1)} %get-tuple-element.15, pred[512,512]{0,1:T(8,128)(4,1)S(1)} %get-tuple-element.33), kind=kOutput, calls=%fused_computation.26 | convolution fusion | flops 681574400 | bytes 13651968 | tf_op jit(solution)/shard_map/gjqk,kgd->gjqd/dot_general | solution.py:66
  205.7 2.2 fusion.8
  208.0 0.2 copy-done.8
  208.2 0.8 copy-done.9
  209.0 5.1 %fusion.34 = bf16[512,2,5,128]{0,3,2,1:T(8,128)(2,1)S(1)} fusion(f32[2,5,512,128]{2,3,1,0:T(8,128)} %fusion.17, f32[2,5,512,128]{2,3,1,0:T(8,128)S(1)} %copy-done.9, f32[2,5,512,128]{2,3,1,0:T(8,128)S(1)} %copy-done.8, f32[2,5,512,128]{2,3,1,0:T(8,128)S(1)} %copy-done.7, bf16[512,2,128,1]{0,2,3,1:T(8,128)(2,1)S(1)} %bitcast.275, ...), kind=kOutput, calls=%fused_computation.42 | convolution fusion | flops 688783360 | bytes 22949888 | tf_op jit(solution)/shard_map/gjqk,kgd->gjqd/dot_general | solution.py:66
  214.1 1.4 copy.68
  (42 shorter events, 0.2 us)
Async XLA Ops:
  6.5 16.6 %copy-start.6 = (f32[2,256]{1,0:T(2,128)S(1)}, f32[2,256]{1,0:T(2,128)}, u32[]{:S(2)}) copy-start(f32[2,256]{1,0:T(2,128)} %param.11) | copy-start | bytes 6148
  6.5 16.6 %copy-start = (bf16[512,1280]{1,0:T(8,128)(2,1)S(1)}, bf16[512,1280]{1,0:T(8,128)(2,1)}, u32[]{:S(2)}) copy-start(bf16[512,1280]{1,0:T(8,128)(2,1)} %param.7) | copy-start | bytes 3932164
  6.5 69.6 %all-gather.4.cloned.1.call-start = ((), (), s32[]{:S(2)}) async-start(), calls=%async_computation | async-start | bytes 6553600 | tf_op jit(solution)/shard_map/all_gather | solution.py:27
  83.1 22.4 %collective-permute-start = (bf16[512,2,256]{0,2,1:T(8,128)(2,1)S(1)}, bf16[512,2,256]{0,2,1:T(8,128)(2,1)S(1)}, u32[]{:S(2)}, u32[]{:S(2)}) collective-permute-start(bf16[512,2,256]{0,2,1:T(8,128)(2,1)S(1)} %bitcast.272), channel_id=1, source_target_pairs={{0,4},{4,8},{8,12},{12,16},{16,20},{20,24},{24,28},{28,32},{32,36}... | collective-permute-start | bytes 1572872 | tf_op jit(solution)/shard_map/ppermute | solution.py:14
  105.5 21.5 %collective-permute-start.1 = (bf16[512,2,256]{0,2,1:T(8,128)(2,1)S(1)}, bf16[512,2,256]{0,2,1:T(8,128)(2,1)S(1)}, u32[]{:S(2)}, u32[]{:S(2)}) collective-permute-start(bf16[512,2,256]{0,2,1:T(8,128)(2,1)S(1)} %collective-permute-done), channel_id=1, source_target_pairs={{0,4},{4,8},{8,12},{12,16},{16,20},{20,24},{24,28},{28,32},{32,36}... | collective-permute-start | bytes 1572872 | tf_op jit(solution)/shard_map/ppermute | solution.py:14
  127.1 20.7 %collective-permute-start.2 = (bf16[512,2,256]{0,2,1:T(8,128)(2,1)S(1)}, bf16[512,2,256]{0,2,1:T(8,128)(2,1)S(1)}, u32[]{:S(2)}, u32[]{:S(2)}) collective-permute-start(bf16[512,2,256]{0,2,1:T(8,128)(2,1)S(1)} %collective-permute-done.1), channel_id=1, source_target_pairs={{0,4},{4,8},{8,12},{12,16},{16,20},{20,24},{24,28},{28,32},{32,36}... | collective-permute-start | bytes 1572872 | tf_op jit(solution)/shard_map/ppermute | solution.py:14
  147.8 19.8 %collective-permute-start.3 = (bf16[512,2,256]{0,2,1:T(8,128)(2,1)S(1)}, bf16[512,2,256]{0,2,1:T(8,128)(2,1)S(1)}, u32[]{:S(2)}, u32[]{:S(2)}) collective-permute-start(bf16[512,2,256]{0,2,1:T(8,128)(2,1)S(1)} %collective-permute-done.2), channel_id=1, source_target_pairs={{0,4},{4,8},{8,12},{12,16},{16,20},{20,24},{24,28},{28,32},{32,36}... | collective-permute-start | bytes 1572872 | tf_op jit(solution)/shard_map/ppermute | solution.py:14
  174.7 7.9 %slice-start = ((s8[10485760]{0:T(1024)(128)(4,1)}), s8[4194304]{0:T(1024)(128)(4,1)S(1)}, s32[]{:S(2)}) async-start(s8[10485760]{0:T(1024)(128)(4,1)} %bitcast.256), calls=%async_computation.1 | async-start | bytes 8388608
  174.7 7.9 %slice-start.1 = ((s8[10485760]{0:T(1024)(128)(4,1)}), s8[4194304]{0:T(1024)(128)(4,1)S(1)}, s32[]{:S(2)}) async-start(s8[10485760]{0:T(1024)(128)(4,1)} %bitcast.256), calls=%async_computation.2 | async-start | bytes 8388608
  176.9 5.7 %slice-start.2 = ((s8[10485760]{0:T(1024)(128)(4,1)}), s8[2097152]{0:T(1024)(128)(4,1)S(1)}, s32[]{:S(2)}) async-start(s8[10485760]{0:T(1024)(128)(4,1)} %bitcast.256), calls=%async_computation.3 | async-start | bytes 4194304
  182.6 3.1 %copy-start.2 = (bf16[512,1,256]{0,2,1:T(8,128)(2,1)S(1)}, bf16[512,1,256]{0,2,1:T(8,128)(2,1)}, u32[]{:S(2)}) copy-start(bf16[512,1,256]{0,2,1:T(8,128)(2,1)} %get-tuple-element.22) | copy-start | bytes 786436
  182.6 8.1 %slice-start.6 = ((s8[10485760]{0:T(1024)(128)(4,1)}), s8[4194304]{0:T(1024)(128)(4,1)S(1)}, s32[]{:S(2)}) async-start(s8[10485760]{0:T(1024)(128)(4,1)} %bitcast.260), calls=%async_computation.7 | async-start | bytes 8388608
  182.6 8.1 %slice-start.7 = ((s8[10485760]{0:T(1024)(128)(4,1)}), s8[4194304]{0:T(1024)(128)(4,1)S(1)}, s32[]{:S(2)}) async-start(s8[10485760]{0:T(1024)(128)(4,1)} %bitcast.260), calls=%async_computation.8 | async-start | bytes 8388608
  185.7 5.0 %slice-start.8 = ((s8[10485760]{0:T(1024)(128)(4,1)}), s8[2097152]{0:T(1024)(128)(4,1)S(1)}, s32[]{:S(2)}) async-start(s8[10485760]{0:T(1024)(128)(4,1)} %bitcast.260), calls=%async_computation.9 | async-start | bytes 4194304
  190.7 3.7 %copy-start.3 = (bf16[512,1,256]{0,2,1:T(8,128)(2,1)S(1)}, bf16[512,1,256]{0,2,1:T(8,128)(2,1)}, u32[]{:S(2)}) copy-start(bf16[512,1,256]{0,2,1:T(8,128)(2,1)} %get-tuple-element.24) | copy-start | bytes 786436
  190.7 8.7 %slice-start.9 = ((s8[10485760]{0:T(1024)(128)(4,1)}), s8[4194304]{0:T(1024)(128)(4,1)S(1)}, s32[]{:S(2)}) async-start(s8[10485760]{0:T(1024)(128)(4,1)} %bitcast.262), calls=%async_computation.10 | async-start | bytes 8388608
  190.7 8.7 %slice-start.10 = ((s8[10485760]{0:T(1024)(128)(4,1)}), s8[4194304]{0:T(1024)(128)(4,1)S(1)}, s32[]{:S(2)}) async-start(s8[10485760]{0:T(1024)(128)(4,1)} %bitcast.262), calls=%async_computation.11 | async-start | bytes 8388608
  194.4 5.0 %slice-start.11 = ((s8[10485760]{0:T(1024)(128)(4,1)}), s8[2097152]{0:T(1024)(128)(4,1)S(1)}, s32[]{:S(2)}) async-start(s8[10485760]{0:T(1024)(128)(4,1)} %bitcast.262), calls=%async_computation.12 | async-start | bytes 4194304
  194.4 7.2 %copy-start.4 = (bf16[512,1,256]{0,2,1:T(8,128)(2,1)S(1)}, bf16[512,1,256]{0,2,1:T(8,128)(2,1)}, u32[]{:S(2)}) copy-start(bf16[512,1,256]{0,2,1:T(8,128)(2,1)} %get-tuple-element.27) | copy-start | bytes 786436
  199.4 6.3 %slice-start.3 = ((s8[10485760]{0:T(1024)(128)(4,1)}), s8[4194304]{0:T(1024)(128)(4,1)S(1)}, s32[]{:S(2)}) async-start(s8[10485760]{0:T(1024)(128)(4,1)} %bitcast.258), calls=%async_computation.4 | async-start | bytes 8388608
  199.4 6.3 %slice-start.4 = ((s8[10485760]{0:T(1024)(128)(4,1)}), s8[4194304]{0:T(1024)(128)(4,1)S(1)}, s32[]{:S(2)}) async-start(s8[10485760]{0:T(1024)(128)(4,1)} %bitcast.258), calls=%async_computation.5 | async-start | bytes 8388608
  201.6 4.1 %slice-start.5 = ((s8[10485760]{0:T(1024)(128)(4,1)}), s8[2097152]{0:T(1024)(128)(4,1)S(1)}, s32[]{:S(2)}) async-start(s8[10485760]{0:T(1024)(128)(4,1)} %bitcast.258), calls=%async_computation.6 | async-start | bytes 4194304
  201.6 6.3 %copy-start.5 = (f32[2,5,512]{2,1,0:T(8,128)S(1)}, f32[2,5,512]{2,1,0:T(8,128)}, u32[]{:S(2)}) copy-start(f32[2,5,512]{2,1,0:T(8,128)} %fusion.4) | copy-start | bytes 61444
  201.6 6.4 %copy-start.1 = (bf16[512,1,256]{0,2,1:T(8,128)(2,1)S(1)}, bf16[512,1,256]{0,2,1:T(8,128)(2,1)}, u32[]{:S(2)}) copy-start(bf16[512,1,256]{0,2,1:T(8,128)(2,1)} %get-tuple-element.18) | copy-start | bytes 786436
  205.7 2.3 %copy-start.7 = (f32[2,5,512,128]{2,3,1,0:T(8,128)S(1)}, f32[2,5,512,128]{2,3,1,0:T(8,128)}, u32[]{:S(2)}) copy-start(f32[2,5,512,128]{2,3,1,0:T(8,128)} %fusion.23) | copy-start | bytes 7864324
  205.7 2.5 %copy-start.8 = (f32[2,5,512,128]{2,3,1,0:T(8,128)S(1)}, f32[2,5,512,128]{2,3,1,0:T(8,128)}, u32[]{:S(2)}) copy-start(f32[2,5,512,128]{2,3,1,0:T(8,128)} %fusion.21) | copy-start | bytes 7864324
  205.7 3.3 %copy-start.9 = (f32[2,5,512,128]{2,3,1,0:T(8,128)S(1)}, f32[2,5,512,128]{2,3,1,0:T(8,128)}, u32[]{:S(2)}) copy-start(f32[2,5,512,128]{2,3,1,0:T(8,128)} %fusion.19) | copy-start | bytes 7864324
Sparse Core Ops, SparseCore 0:
  16.4 59.7 all-gather.3
